TPU v7x, 32 devices: a whole 2x2x4 slice. The times are simulated.
32 devices in a mesh: vec: 8 (over z, core), rep: 4 (over y, x).
Axes of the slice: x: 2, y: 2, z: 4, core: 2. Of those that a mesh axis runs over, the one named last changes fastest.
Arguments:
- vectors: bfloat16 [1024, 1024], P('vec'), may hold values from 0 to 2
- pivot_index: int32 [4, 8], P('rep'), may hold values from 0 to 1023
Outputs:
- similarity: bfloat16 [7, 32, 1024, 128], P(None, 'rep', 'vec')
All inputs are finite; a program needn't handle non-finite values.
Results may differ from a plain program's by a relative error of at most 0.011.
Values may be sent and summed in bfloat16 or wider, within the bound.
A program may use at most 64 MiB of HBM per device.

v0:
```python
import math
import jax
import jax.numpy as jnp
from jax import lax
from jax.sharding import PartitionSpec as P

HALF = 3


def from_behind(block, axis, distance):
    devices = range(lax.axis_size(axis))
    route = [((i - distance) % len(devices), i) for i in devices]
    return lax.ppermute(block, axis, route)


def contract(left, right):
    return lax.dot_general(
        left, right, (((1,), (1,)), ((), ())), preferred_element_type=jnp.float32
    )


def on_device(vectors, pivot_index):
    block_rows, fields = vectors.shape
    position = lax.axis_index("vec")
    wanted = pivot_index.reshape(-1) - position * block_rows
    columns = jnp.arange(block_rows, dtype=jnp.int32)
    onehot = (wanted[:, None] == columns[None, :]).astype(jnp.bfloat16)
    local_rows = jnp.dot(onehot, vectors, preferred_element_type=jnp.float32)
    pivots = lax.psum(local_rows, "vec")
    count = pivots.shape[0]
    centre = jnp.sum(pivots, axis=1) / fields
    scaled = (vectors.astype(jnp.float32)[None, :, :] * pivots[:, None, :]).astype(jnp.bfloat16)
    scaled = scaled.reshape(count * block_rows, fields)
    replicas = lax.axis_size("rep")
    share = block_rows // replicas
    own_rows = lax.dynamic_slice_in_dim(vectors, lax.axis_index("rep") * share, share, 0)
    window = 2 * HALF + 1
    triples = [None] * window
    grams = [None] * window
    triples[HALF] = contract(scaled, vectors)
    grams[HALF] = contract(own_rows, vectors)
    lower = vectors
    upper = vectors
    for reach in range(1, HALF + 1):
        lower = from_behind(lower, "vec", 1)
        upper = from_behind(upper, "vec", -1)
        triples[HALF - reach] = contract(scaled, lower)
        grams[HALF - reach] = contract(own_rows, lower)
        triples[HALF + reach] = contract(scaled, upper)
        grams[HALF + reach] = contract(own_rows, upper)
    triple_all = jnp.stack(triples).reshape(window, count, block_rows, block_rows)
    gram_all = jnp.stack(grams)
    gram_all = lax.all_gather(gram_all, "rep", axis=1, tiled=True)
    similarity = (triple_all - centre[None, :, None, None] * gram_all[:, None, :, :]) / math.sqrt(
        fields
    )
    return similarity.astype(jnp.bfloat16)


def solution(mesh):
    in_specs = (P("vec", None), P("rep", None))
    out_specs = P(None, "rep", "vec", None)
    return jax.shard_map(
        on_device, mesh=mesh, in_specs=in_specs, out_specs=out_specs, check_vma=False
    )
```

profile of v0, /device:TPU:0, one launch (start us, length us, event | category | flops | bytes accessed | tf_op | source)
XLA Modules:
  0.0 71.4 jit_solution(5123657337619987184)
XLA Ops:
  0.0 0.5 collective-permute-start
  0.5 4.0 %collective-permute-start.3 = (bf16[128,1024]{1,0:T(8,128)(2,1)}, bf16[128,1024]{1,0:T(8,128)(2,1)S(1)}, u32[]{:S(2)}, u32[]{:S(2)}) collective-permute-start(bf16[128,1024]{1,0:T(8,128)(2,1)} %param.2), channel_id=1, source_target_pairs={{4,0},{8,4},{12,8},{16,12},{20,16},{24,20},{28,24},{0,28},{5,1},{9... | collective-permute-start | bytes 786440 | tf_op jit(solution)/shard_map/ppermute | solution.py:13
  4.5 4.5 %collective-permute-done = bf16[128,1024]{1,0:T(8,128)(2,1)S(1)} collective-permute-done((bf16[128,1024]{1,0:T(8,128)(2,1)}, bf16[128,1024]{1,0:T(8,128)(2,1)S(1)}, u32[]{:S(2)}, u32[]{:S(2)}) %collective-permute-start) | collective-permute-done | bytes 262176 | tf_op jit(solution)/shard_map/ppermute | solution.py:13
  9.0 0.7 subtract_bitcast_fusion
  9.7 3.5 %collective-permute-start.4 = (bf16[128,1024]{1,0:T(8,128)(2,1)S(1)}, bf16[128,1024]{1,0:T(8,128)(2,1)S(1)}, u32[]{:S(2)}, u32[]{:S(2)}) collective-permute-start(bf16[128,1024]{1,0:T(8,128)(2,1)S(1)} %collective-permute-done.3), channel_id=1, source_target_pairs={{4,0},{8,4},{12,8},{16,12},{20,16},{24,20},{28,24},{0,28},{5,1},{9... | collective-permute-start | bytes 786440 | tf_op jit(solution)/shard_map/ppermute | solution.py:13
  13.2 3.5 %collective-permute-done.1 = bf16[128,1024]{1,0:T(8,128)(2,1)S(1)} collective-permute-done((bf16[128,1024]{1,0:T(8,128)(2,1)S(1)}, bf16[128,1024]{1,0:T(8,128)(2,1)S(1)}, u32[]{:S(2)}, u32[]{:S(2)}) %collective-permute-start.1) | collective-permute-done | bytes 262176 | tf_op jit(solution)/shard_map/ppermute | solution.py:13
  16.7 1.1 %fusion.56 = f32[8,1024]{1,0:T(8,128)S(1)} fusion(bf16[128,1024]{1,0:T(8,128)(2,1)} %param.2, s32[8]{0:T(128)S(1)} %subtract_bitcast_fusion), kind=kOutput, calls=%fused_computation.66 | convolution fusion | flops 2098176 | bytes 294944 | tf_op jit(solution)/shard_map/dot_general | solution.py:28
  17.8 1.0 %convert_element_type.21 = f32[128,1024]{1,0:T(8,128)S(1)} convert(bf16[128,1024]{1,0:T(8,128)(2,1)} %param.2) | non-fusion elementwise | flops 131072 | bytes 786432 | tf_op jit(solution)/shard_map/convert_element_type | solution.py:32
  18.8 29.4 %psum.7 = f32[8,1024]{1,0:T(8,128)S(1)} all-reduce(f32[8,1024]{1,0:T(8,128)S(1)} %fusion.56), channel_id=1, replica_groups=mesh['vec'=8,'rep'=4] {'vec'}, use_global_device_ids=true, to_apply=%region_0.0 | all-reduce | flops 8192 | bytes 65536 | tf_op jit(solution)/shard_map/psum | solution.py:29
  48.5 1.0 %fusion.41 = f32[7,32,128]{2,1,0:T(8,128)S(1)} fusion(bf16[128,1024]{1,0:T(8,128)(2,1)S(1)} %collective-permute-done.2, bf16[128,1024]{1,0:T(8,128)(2,1)} %param.2, s32[]{:T(128)S(6)} %select_n.3), kind=kOutput, calls=%fused_computation.50 | convolution fusion | flops 8388607 | bytes 344068 | tf_op jit(solution)/shard_map/dot_general | solution.py:17
  49.5 1.0 %fusion.40 = f32[7,32,128]{2,1,0:T(8,128)S(1)} fusion(f32[7,32,128]{2,1,0:T(8,128)S(1)} %fusion.41, bf16[128,1024]{1,0:T(8,128)(2,1)S(1)} %collective-permute-done.1, bf16[128,1024]{1,0:T(8,128)(2,1)} %param.2, s32[]{:T(128)S(6)} %select_n.3), kind=kOutput, calls=%fused_computation.48 | convolution fusion | flops 8388608 | bytes 344068 | tf_op jit(solution)/shard_map/dot_general | solution.py:17
  50.5 1.0 %fusion.39 = f32[7,32,128]{2,1,0:T(8,128)S(1)} fusion(f32[7,32,128]{2,1,0:T(8,128)S(1)} %fusion.40, bf16[128,1024]{1,0:T(8,128)(2,1)S(1)} %collective-permute-done, bf16[128,1024]{1,0:T(8,128)(2,1)} %param.2, s32[]{:T(128)S(6)} %select_n.3), kind=kOutput, calls=%fused_computation.46 | convolution fusion | flops 8388608 | bytes 344068 | tf_op jit(solution)/shard_map/dot_general | solution.py:17
  51.6 1.2 %fusion.38 = f32[7,32,128]{2,1,0:T(8,128)S(1)} fusion(f32[7,32,128]{2,1,0:T(8,128)S(1)} %fusion.39, bf16[128,1024]{1,0:T(8,128)(2,1)} %param.2, s32[]{:T(128)S(6)} %select_n.3), kind=kOutput, calls=%fused_computation.44 | convolution fusion | flops 8388608 | bytes 344068 | tf_op jit(solution)/shard_map/dot_general | solution.py:17
  52.8 0.7 %fusion.22 = f32[7,8,128,128]{3,2,1,0:T(8,128)S(1)} fusion(f32[8,1024]{1,0:T(8,128)S(1)} %psum.7, f32[128,1024]{1,0:T(8,128)S(1)} %convert_element_type.21, bf16[128,1024]{1,0:T(8,128)(2,1)S(1)} %collective-permute-done.2), kind=kOutput, calls=%fused_computation.24 | convolution fusion | flops 270532608 | bytes 1343488 | tf_op jit(solution)/shard_map/dot_general | solution.py:17
  53.6 0.7 fusion.24
  54.3 0.7 fusion.26
  55.2 0.2 fusion.36
  55.4 0.7 %fusion.28 = f32[7,8,128,128]{3,2,1,0:T(8,128)S(1)} fusion(f32[7,8,128,128]{3,2,1,0:T(8,128)S(1)} %fusion.26, f32[8,1024]{1,0:T(8,128)S(1)} %psum.7, f32[128,1024]{1,0:T(8,128)S(1)} %convert_element_type.21, bf16[128,1024]{1,0:T(8,128)(2,1)S(1)} %copy-done), kind=kOutput, calls=%fused_computation.30 | convolution fusion | flops 270532608 | bytes 1343488 | tf_op jit(solution)/shard_map/dot_general | solution.py:17
  56.1 0.2 fusion.35
  56.3 11.0 %all_gather.3 = f32[7,128,128]{2,1,0:T(8,128)S(1)} all-gather(f32[7,32,128]{2,1,0:T(8,128)S(1)} %fusion.35), channel_id=1, replica_groups=mesh['vec'=8,'rep'=4] {'rep'}, dimensions={1}, use_global_device_ids=true | all-gather | bytes 573440 | tf_op jit(solution)/shard_map/all_gather | solution.py:53
  67.3 0.7 fusion.30
  68.0 0.7 fusion.32
  68.8 0.7 fusion.34
  69.5 1.9 %multiply_convert_fusion.8 = bf16[7,8,128,128]{3,2,1,0:T(8,128)(2,1)} fusion(f32[7,8,128,128]{3,2,1,0:T(8,128)S(1)} %fusion.34, f32[7,128,128]{2,1,0:T(8,128)S(1)} %all_gather.3, f32[8]{0:T(128)S(1)} %broadcast_multiply_fusion), kind=kLoop, calls=%fused_computation.8 | loop fusion | flops 3670016 | bytes 5963808 | tf_op jit(solution)/shard_map/convert_element_type | solution.py:57
  (12 shorter events, 0.4 us)
Async XLA Ops:
  0.0 9.0 %collective-permute-start = (bf16[128,1024]{1,0:T(8,128)(2,1)}, bf16[128,1024]{1,0:T(8,128)(2,1)S(1)}, u32[]{:S(2)}, u32[]{:S(2)}) collective-permute-start(bf16[128,1024]{1,0:T(8,128)(2,1)} %param.2), channel_id=1, source_target_pairs={{28,0},{0,4},{4,8},{8,12},{12,16},{16,20},{20,24},{24,28},{29,1},{... | collective-permute-start | bytes 786440 | tf_op jit(solution)/shard_map/ppermute | solution.py:13
  0.5 9.2 %collective-permute-start.3 = (bf16[128,1024]{1,0:T(8,128)(2,1)}, bf16[128,1024]{1,0:T(8,128)(2,1)S(1)}, u32[]{:S(2)}, u32[]{:S(2)}) collective-permute-start(bf16[128,1024]{1,0:T(8,128)(2,1)} %param.2), channel_id=1, source_target_pairs={{4,0},{8,4},{12,8},{16,12},{20,16},{24,20},{28,24},{0,28},{5,1},{9... | collective-permute-start | bytes 786440 | tf_op jit(solution)/shard_map/ppermute | solution.py:13
  9.0 7.7 %collective-permute-start.1 = (bf16[128,1024]{1,0:T(8,128)(2,1)S(1)}, bf16[128,1024]{1,0:T(8,128)(2,1)S(1)}, u32[]{:S(2)}, u32[]{:S(2)}) collective-permute-start(bf16[128,1024]{1,0:T(8,128)(2,1)S(1)} %collective-permute-done), channel_id=1, source_target_pairs={{28,0},{0,4},{4,8},{8,12},{12,16},{16,20},{20,24},{24,28},{29,1},{... | collective-permute-start | bytes 786440 | tf_op jit(solution)/shard_map/ppermute | solution.py:13
  9.7 38.7 %collective-permute-start.4 = (bf16[128,1024]{1,0:T(8,128)(2,1)S(1)}, bf16[128,1024]{1,0:T(8,128)(2,1)S(1)}, u32[]{:S(2)}, u32[]{:S(2)}) collective-permute-start(bf16[128,1024]{1,0:T(8,128)(2,1)S(1)} %collective-permute-done.3), channel_id=1, source_target_pairs={{4,0},{8,4},{12,8},{16,12},{20,16},{24,20},{28,24},{0,28},{5,1},{9... | collective-permute-start | bytes 786440 | tf_op jit(solution)/shard_map/ppermute | solution.py:13
  16.7 31.8 %collective-permute-start.2 = (bf16[128,1024]{1,0:T(8,128)(2,1)S(1)}, bf16[128,1024]{1,0:T(8,128)(2,1)S(1)}, u32[]{:S(2)}, u32[]{:S(2)}) collective-permute-start(bf16[128,1024]{1,0:T(8,128)(2,1)S(1)} %collective-permute-done.1), channel_id=1, source_target_pairs={{28,0},{0,4},{4,8},{8,12},{12,16},{16,20},{20,24},{24,28},{29,1},{... | collective-permute-start | bytes 786440 | tf_op jit(solution)/shard_map/ppermute | solution.py:13
  48.4 7.7 %collective-permute-start.5 = (bf16[128,1024]{1,0:T(8,128)(2,1)S(1)}, bf16[128,1024]{1,0:T(8,128)(2,1)S(1)}, u32[]{:S(2)}, u32[]{:S(2)}) collective-permute-start(bf16[128,1024]{1,0:T(8,128)(2,1)S(1)} %collective-permute-done.4), channel_id=1, source_target_pairs={{4,0},{8,4},{12,8},{16,12},{20,16},{24,20},{28,24},{0,28},{5,1},{9... | collective-permute-start | bytes 786440 | tf_op jit(solution)/shard_map/ppermute | solution.py:13
  52.8 2.2 %copy-start = (bf16[128,1024]{1,0:T(8,128)(2,1)S(1)}, bf16[128,1024]{1,0:T(8,128)(2,1)}, u32[]{:S(2)}) copy-start(bf16[128,1024]{1,0:T(8,128)(2,1)} %param.2) | copy-start | bytes 786436
where the time goes:
time: 71.7 us; the launch traced here: 71.4 us
  blocking collectives  40.5 us (56%)
  matrix products  11 us (15%)
  starting transfers between devices  8.13 us (11%)
  waiting for transfers between devices  7.96 us (11%)
  other arithmetic  3.69 us (5%)
    psum x1, blocking collectives, on_device(): pivots = lax.psum(local_rows, 'vec')  29.4 us
    all_gather x1, blocking collectives, on_device(): gram_all = lax.all_gather(gram_all, 'rep', axis=1, tiled=True)  11 us
    dot_general x14, matrix products, contract(): lax.dot_general(left, right, (((1,), (1,)), ((), ())), preferred_element_...  9.87 us
    ppermute x6, starting transfers between devices, from_behind(): return lax.ppermute(block, axis, route)  8.13 us
    ppermute x6, waiting for transfers between devices, from_behind(): return lax.ppermute(block, axis, route)  7.96 us
    convert_element_type x1, other arithmetic, on_device(): return similarity.astype(jnp.bfloat16)  1.9 us
  transfers between devices with their start and end apart: 6, of which 2 were waited for; matrix products, arithmetic and copies ran while one was open for 15% of the time, Pallas kernels for 0%

commit v1 on v0

--- a/solution.py
+++ b/solution.py
@@ -26,7 +26,7 @@
     columns = jnp.arange(block_rows, dtype=jnp.int32)
     onehot = (wanted[:, None] == columns[None, :]).astype(jnp.bfloat16)
     local_rows = jnp.dot(onehot, vectors, preferred_element_type=jnp.float32)
-    pivots = lax.psum(local_rows, "vec")
+    pivots = jnp.sum(lax.all_gather(local_rows, "vec"), axis=0)
     count = pivots.shape[0]
     centre = jnp.sum(pivots, axis=1) / fields
     scaled = (vectors.astype(jnp.float32)[None, :, :] * pivots[:, None, :]).astype(jnp.bfloat16)

time: 71.7 us -> 60.8 us (0.85)
  blocking collectives: 40.5 us -> 25.6 us
  starting transfers between devices: 8.13 us -> 11.5 us
  matrix products: 11 us -> 11.8 us
    psum x1 -> x0, blocking collectives: 29.4 us -> none  [on_device(): pivots = lax.psum(local_rows, 'vec')]
    all_gather x0 -> x1, blocking collectives: none -> 15.8 us  [on_device(): pivots = jnp.sum(lax.all_gather(local_rows, 'vec'), axis=0)]
    ppermute x6, starting transfers between devices: 8.13 us -> 11.5 us  [from_behind(): return lax.ppermute(block, axis, route)]
    all_gather x1, blocking collectives: 11 us -> 9.8 us  [on_device(): gram_all = lax.all_gather(gram_all, 'rep', axis=1, tiled=True)]
    dot_general x14, matrix products: 9.87 us -> 10.7 us  [contract(): lax.dot_general(left, right, (((1,), (1,)), ((), ())), preferred_element_...]
  transfers between devices with their start and end apart: 6 -> 6, of which waited for: 2 -> 2; matrix products, arithmetic and copies ran while one was open for 15% -> 14% of each run, Pallas kernels for 0% -> 0%
where the time goes in v1:
time: 60.8 us; the launch traced here: 60.3 us
  blocking collectives  25.6 us (42%)
  matrix products  11.8 us (19%)
  starting transfers between devices  11.5 us (19%)
  waiting for transfers between devices  7.57 us (12%)
  other arithmetic  3.72 us (6%)
    all_gather x1, blocking collectives, on_device(): pivots = jnp.sum(lax.all_gather(local_rows, 'vec'), axis=0)  15.8 us
    ppermute x6, starting transfers between devices, from_behind(): return lax.ppermute(block, axis, route)  11.5 us
    dot_general x14, matrix products, contract(): lax.dot_general(left, right, (((1,), (1,)), ((), ())), preferred_element_...  10.7 us
    all_gather x1, blocking collectives, on_device(): gram_all = lax.all_gather(gram_all, 'rep', axis=1, tiled=True)  9.8 us
    ppermute x6, waiting for transfers between devices, from_behind(): return lax.ppermute(block, axis, route)  7.57 us
    convert_element_type x1, other arithmetic, on_device(): return similarity.astype(jnp.bfloat16)  1.9 us
  transfers between devices with their start and end apart: 6, of which 2 were waited for; matrix products, arithmetic and copies ran while one was open for 14% of the time, Pallas kernels for 0%

profile of v1, /device:TPU:0, one launch (start us, length us, event | category | flops | bytes accessed | tf_op | source)
XLA Modules:
  0.0 60.3 jit_solution(16454567291798074703)
XLA Ops:
  0.0 0.5 collective-permute-start
  0.5 4.1 %collective-permute-start.3 = (bf16[128,1024]{1,0:T(8,128)(2,1)}, bf16[128,1024]{1,0:T(8,128)(2,1)S(1)}, u32[]{:S(2)}, u32[]{:S(2)}) collective-permute-start(bf16[128,1024]{1,0:T(8,128)(2,1)} %param.2), channel_id=1, source_target_pairs={{4,0},{8,4},{12,8},{16,12},{20,16},{24,20},{28,24},{0,28},{5,1},{9... | collective-permute-start | bytes 786440 | tf_op jit(solution)/shard_map/ppermute | solution.py:13
  4.6 0.7 %subtract_bitcast_fusion = s32[8]{0:T(128)S(1)} fusion(s32[1,8]{1,0:T(1,128)} %param.3, s32[]{:T(128)S(6)} %mul.44), kind=kLoop, calls=%fused_computation.69 | loop fusion | flops 8 | bytes 68 | tf_op jit(solution)/shard_map/sub | solution.py:25
  5.2 3.9 %collective-permute-done = bf16[128,1024]{1,0:T(8,128)(2,1)S(1)} collective-permute-done((bf16[128,1024]{1,0:T(8,128)(2,1)}, bf16[128,1024]{1,0:T(8,128)(2,1)S(1)}, u32[]{:S(2)}, u32[]{:S(2)}) %collective-permute-start) | collective-permute-done | bytes 262176 | tf_op jit(solution)/shard_map/ppermute | solution.py:13
  9.1 1.1 %fusion.56 = f32[8,1024]{1,0:T(8,128)S(1)} fusion(bf16[128,1024]{1,0:T(8,128)(2,1)} %param.2, s32[8]{0:T(128)S(1)} %subtract_bitcast_fusion), kind=kOutput, calls=%fused_computation.67 | convolution fusion | flops 2098176 | bytes 294944 | tf_op jit(solution)/shard_map/dot_general | solution.py:28
  10.3 15.8 %all-gather = f32[64,1024]{1,0:T(8,128)S(1)} all-gather(f32[8,1024]{1,0:T(8,128)S(1)} %fusion.56), channel_id=2, replica_groups=mesh['vec'=8,'rep'=4] {'vec'}, dimensions={0}, use_global_device_ids=true | all-gather | bytes 294912 | tf_op jit(solution)/shard_map/all_gather | solution.py:29
  26.1 3.2 %collective-permute-start.4 = (bf16[128,1024]{1,0:T(8,128)(2,1)S(1)}, bf16[128,1024]{1,0:T(8,128)(2,1)S(1)}, u32[]{:S(2)}, u32[]{:S(2)}) collective-permute-start(bf16[128,1024]{1,0:T(8,128)(2,1)S(1)} %collective-permute-done.3), channel_id=1, source_target_pairs={{4,0},{8,4},{12,8},{16,12},{20,16},{24,20},{28,24},{0,28},{5,1},{9... | collective-permute-start | bytes 786440 | tf_op jit(solution)/shard_map/ppermute | solution.py:13
  29.3 1.0 %convert_element_type.21 = f32[128,1024]{1,0:T(8,128)S(1)} convert(bf16[128,1024]{1,0:T(8,128)(2,1)} %param.2) | non-fusion elementwise | flops 131072 | bytes 786432 | tf_op jit(solution)/shard_map/convert_element_type | solution.py:32
  30.5 3.7 %collective-permute-done.4 = bf16[128,1024]{1,0:T(8,128)(2,1)S(1)} collective-permute-done((bf16[128,1024]{1,0:T(8,128)(2,1)S(1)}, bf16[128,1024]{1,0:T(8,128)(2,1)S(1)}, u32[]{:S(2)}, u32[]{:S(2)}) %collective-permute-start.4) | collective-permute-done | bytes 262176 | tf_op jit(solution)/shard_map/ppermute | solution.py:13
  34.2 3.7 %collective-permute-start.5 = (bf16[128,1024]{1,0:T(8,128)(2,1)S(1)}, bf16[128,1024]{1,0:T(8,128)(2,1)S(1)}, u32[]{:S(2)}, u32[]{:S(2)}) collective-permute-start(bf16[128,1024]{1,0:T(8,128)(2,1)S(1)} %collective-permute-done.4), channel_id=1, source_target_pairs={{4,0},{8,4},{12,8},{16,12},{20,16},{24,20},{28,24},{0,28},{5,1},{9... | collective-permute-start | bytes 786440 | tf_op jit(solution)/shard_map/ppermute | solution.py:13
  37.9 1.0 %fusion.41 = f32[7,32,128]{2,1,0:T(8,128)S(1)} fusion(bf16[128,1024]{1,0:T(8,128)(2,1)S(1)} %collective-permute-done.2, bf16[128,1024]{1,0:T(8,128)(2,1)} %param.2, s32[]{:T(128)S(6)} %select_n.3), kind=kOutput, calls=%fused_computation.50 | convolution fusion | flops 8388607 | bytes 344068 | tf_op jit(solution)/shard_map/dot_general | solution.py:17
  38.9 1.0 %fusion.40 = f32[7,32,128]{2,1,0:T(8,128)S(1)} fusion(f32[7,32,128]{2,1,0:T(8,128)S(1)} %fusion.41, bf16[128,1024]{1,0:T(8,128)(2,1)S(1)} %collective-permute-done.1, bf16[128,1024]{1,0:T(8,128)(2,1)} %param.2, s32[]{:T(128)S(6)} %select_n.3), kind=kOutput, calls=%fused_computation.48 | convolution fusion | flops 8388608 | bytes 344068 | tf_op jit(solution)/shard_map/dot_general | solution.py:17
  39.9 1.0 %fusion.39 = f32[7,32,128]{2,1,0:T(8,128)S(1)} fusion(f32[7,32,128]{2,1,0:T(8,128)S(1)} %fusion.40, bf16[128,1024]{1,0:T(8,128)(2,1)S(1)} %collective-permute-done, bf16[128,1024]{1,0:T(8,128)(2,1)} %param.2, s32[]{:T(128)S(6)} %select_n.3), kind=kOutput, calls=%fused_computation.46 | convolution fusion | flops 8388608 | bytes 344068 | tf_op jit(solution)/shard_map/dot_general | solution.py:17
  41.0 1.2 %fusion.38 = f32[7,32,128]{2,1,0:T(8,128)S(1)} fusion(f32[7,32,128]{2,1,0:T(8,128)S(1)} %fusion.39, bf16[128,1024]{1,0:T(8,128)(2,1)} %param.2, s32[]{:T(128)S(6)} %select_n.3), kind=kOutput, calls=%fused_computation.44 | convolution fusion | flops 8388608 | bytes 344068 | tf_op jit(solution)/shard_map/dot_general | solution.py:17
  42.2 1.0 %fusion.37 = f32[7,32,128]{2,1,0:T(8,128)S(1)} fusion(f32[7,32,128]{2,1,0:T(8,128)S(1)} %fusion.38, bf16[128,1024]{1,0:T(8,128)(2,1)S(1)} %collective-permute-done.3, bf16[128,1024]{1,0:T(8,128)(2,1)} %param.2, s32[]{:T(128)S(6)} %select_n.3), kind=kOutput, calls=%fused_computation.42 | convolution fusion | flops 8388608 | bytes 344068 | tf_op jit(solution)/shard_map/dot_general | solution.py:17
  43.6 9.8 %all_gather.11 = f32[7,128,128]{2,1,0:T(8,128)S(1)} all-gather(f32[7,32,128]{2,1,0:T(8,128)S(1)} %fusion.35), channel_id=1, replica_groups=mesh['vec'=8,'rep'=4] {'rep'}, dimensions={1}, use_global_device_ids=true | all-gather | bytes 573440 | tf_op jit(solution)/shard_map/all_gather | solution.py:53
  53.4 0.7 %fusion.22 = f32[7,8,128,128]{3,2,1,0:T(8,128)S(1)} fusion(f32[8,1024]{1,0:T(8,128)S(1)} %bitcast_reduce_fusion, f32[128,1024]{1,0:T(8,128)S(1)} %convert_element_type.21, bf16[128,1024]{1,0:T(8,128)(2,1)S(1)} %collective-permute-done.2), kind=kOutput, calls=%fused_computation.24 | convolution fusion | flops 270532608 | bytes 1343488 | tf_op jit(solution)/shard_map/dot_general | solution.py:17
  54.2 0.7 %fusion.24 = f32[7,8,128,128]{3,2,1,0:T(8,128)S(1)} fusion(f32[7,8,128,128]{3,2,1,0:T(8,128)S(1)} %fusion.22, f32[8,1024]{1,0:T(8,128)S(1)} %bitcast_reduce_fusion, f32[128,1024]{1,0:T(8,128)S(1)} %convert_element_type.21, bf16[128,1024]{1,0:T(8,128)(2,1)S(1)} %collective-permute-done.1), kind=kOutput, calls=%fused_computation.26 | convolution fusion | flops 270532608 | bytes 1343488 | tf_op jit(solution)/shard_map/dot_general | solution.py:17
  54.9 0.7 %fusion.26 = f32[7,8,128,128]{3,2,1,0:T(8,128)S(1)} fusion(f32[7,8,128,128]{3,2,1,0:T(8,128)S(1)} %fusion.24, f32[8,1024]{1,0:T(8,128)S(1)} %bitcast_reduce_fusion, f32[128,1024]{1,0:T(8,128)S(1)} %convert_element_type.21, bf16[128,1024]{1,0:T(8,128)(2,1)S(1)} %collective-permute-done), kind=kOutput, calls=%fused_computation.28 | convolution fusion | flops 270532608 | bytes 1343488 | tf_op jit(solution)/shard_map/dot_general | solution.py:17
  55.6 0.7 %fusion.28 = f32[7,8,128,128]{3,2,1,0:T(8,128)S(1)} fusion(f32[7,8,128,128]{3,2,1,0:T(8,128)S(1)} %fusion.26, f32[8,1024]{1,0:T(8,128)S(1)} %bitcast_reduce_fusion, f32[128,1024]{1,0:T(8,128)S(1)} %convert_element_type.21, bf16[128,1024]{1,0:T(8,128)(2,1)S(1)} %copy-done), kind=kOutput, calls=%fused_computation.30 | convolution fusion | flops 270532608 | bytes 1343488 | tf_op jit(solution)/shard_map/dot_general | solution.py:17
  56.3 0.7 %fusion.30 = f32[7,8,128,128]{3,2,1,0:T(8,128)S(1)} fusion(f32[7,8,128,128]{3,2,1,0:T(8,128)S(1)} %fusion.28, f32[8,1024]{1,0:T(8,128)S(1)} %bitcast_reduce_fusion, f32[128,1024]{1,0:T(8,128)S(1)} %convert_element_type.21, bf16[128,1024]{1,0:T(8,128)(2,1)S(1)} %collective-permute-done.3), kind=kOutput, calls=%fused_computation.32 | convolution fusion | flops 270532608 | bytes 1343488 | tf_op jit(solution)/shard_map/dot_general | solution.py:17
  57.0 0.7 %fusion.32 = f32[7,8,128,128]{3,2,1,0:T(8,128)S(1)} fusion(f32[7,8,128,128]{3,2,1,0:T(8,128)S(1)} %fusion.30, f32[8,1024]{1,0:T(8,128)S(1)} %bitcast_reduce_fusion, f32[128,1024]{1,0:T(8,128)S(1)} %convert_element_type.21, bf16[128,1024]{1,0:T(8,128)(2,1)S(1)} %collective-permute-done.4), kind=kOutput, calls=%fused_computation.34 | convolution fusion | flops 270532608 | bytes 1343488 | tf_op jit(solution)/shard_map/dot_general | solution.py:17
  57.7 0.7 %fusion.34 = f32[7,8,128,128]{3,2,1,0:T(8,128)S(1)} fusion(f32[7,8,128,128]{3,2,1,0:T(8,128)S(1)} %fusion.32, f32[8,1024]{1,0:T(8,128)S(1)} %bitcast_reduce_fusion, f32[128,1024]{1,0:T(8,128)S(1)} %convert_element_type.21, bf16[128,1024]{1,0:T(8,128)(2,1)S(1)} %collective-permute-done.5), kind=kOutput, calls=%fused_computation.36 | convolution fusion | flops 270532608 | bytes 1343488 | tf_op jit(solution)/shard_map/dot_general | solution.py:17
  58.4 1.9 %multiply_convert_fusion.8 = bf16[7,8,128,128]{3,2,1,0:T(8,128)(2,1)} fusion(f32[7,8,128,128]{3,2,1,0:T(8,128)S(1)} %fusion.34, f32[7,128,128]{2,1,0:T(8,128)S(1)} %all_gather.11, f32[8]{0:T(128)S(1)} %broadcast_multiply_fusion), kind=kLoop, calls=%fused_computation.8 | loop fusion | flops 3670016 | bytes 5963808 | tf_op jit(solution)/shard_map/convert_element_type | solution.py:57
  (15 shorter events, 0.6 us)
Async XLA Ops:
  0.0 43.2 %copy-start = (bf16[128,1024]{1,0:T(8,128)(2,1)S(1)}, bf16[128,1024]{1,0:T(8,128)(2,1)}, u32[]{:S(2)}) copy-start(bf16[128,1024]{1,0:T(8,128)(2,1)} %param.2) | copy-start | bytes 786436
  0.0 9.1 %collective-permute-start = (bf16[128,1024]{1,0:T(8,128)(2,1)}, bf16[128,1024]{1,0:T(8,128)(2,1)S(1)}, u32[]{:S(2)}, u32[]{:S(2)}) collective-permute-start(bf16[128,1024]{1,0:T(8,128)(2,1)} %param.2), channel_id=1, source_target_pairs={{28,0},{0,4},{4,8},{8,12},{12,16},{16,20},{20,24},{24,28},{29,1},{... | collective-permute-start | bytes 786440 | tf_op jit(solution)/shard_map/ppermute | solution.py:13
  0.5 25.6 %collective-permute-start.3 = (bf16[128,1024]{1,0:T(8,128)(2,1)}, bf16[128,1024]{1,0:T(8,128)(2,1)S(1)}, u32[]{:S(2)}, u32[]{:S(2)}) collective-permute-start(bf16[128,1024]{1,0:T(8,128)(2,1)} %param.2), channel_id=1, source_target_pairs={{4,0},{8,4},{12,8},{16,12},{20,16},{24,20},{28,24},{0,28},{5,1},{9... | collective-permute-start | bytes 786440 | tf_op jit(solution)/shard_map/ppermute | solution.py:13
  9.1 20.1 %collective-permute-start.1 = (bf16[128,1024]{1,0:T(8,128)(2,1)S(1)}, bf16[128,1024]{1,0:T(8,128)(2,1)S(1)}, u32[]{:S(2)}, u32[]{:S(2)}) collective-permute-start(bf16[128,1024]{1,0:T(8,128)(2,1)S(1)} %collective-permute-done), channel_id=1, source_target_pairs={{28,0},{0,4},{4,8},{8,12},{12,16},{16,20},{20,24},{24,28},{29,1},{... | collective-permute-start | bytes 786440 | tf_op jit(solution)/shard_map/ppermute | solution.py:13
  26.1 8.1 %collective-permute-start.4 = (bf16[128,1024]{1,0:T(8,128)(2,1)S(1)}, bf16[128,1024]{1,0:T(8,128)(2,1)S(1)}, u32[]{:S(2)}, u32[]{:S(2)}) collective-permute-start(bf16[128,1024]{1,0:T(8,128)(2,1)S(1)} %collective-permute-done.3), channel_id=1, source_target_pairs={{4,0},{8,4},{12,8},{16,12},{20,16},{24,20},{28,24},{0,28},{5,1},{9... | collective-permute-start | bytes 786440 | tf_op jit(solution)/shard_map/ppermute | solution.py:13
  29.2 8.6 %collective-permute-start.2 = (bf16[128,1024]{1,0:T(8,128)(2,1)S(1)}, bf16[128,1024]{1,0:T(8,128)(2,1)S(1)}, u32[]{:S(2)}, u32[]{:S(2)}) collective-permute-start(bf16[128,1024]{1,0:T(8,128)(2,1)S(1)} %collective-permute-done.1), channel_id=1, source_target_pairs={{28,0},{0,4},{4,8},{8,12},{12,16},{16,20},{20,24},{24,28},{29,1},{... | collective-permute-start | bytes 786440 | tf_op jit(solution)/shard_map/ppermute | solution.py:13
  34.2 9.3 %collective-permute-start.5 = (bf16[128,1024]{1,0:T(8,128)(2,1)S(1)}, bf16[128,1024]{1,0:T(8,128)(2,1)S(1)}, u32[]{:S(2)}, u32[]{:S(2)}) collective-permute-start(bf16[128,1024]{1,0:T(8,128)(2,1)S(1)} %collective-permute-done.4), channel_id=1, source_target_pairs={{4,0},{8,4},{12,8},{16,12},{20,16},{24,20},{28,24},{0,28},{5,1},{9... | collective-permute-start | bytes 786440 | tf_op jit(solution)/shard_map/ppermute | solution.py:13
